TPU v7x, 256 devices: a whole 4x4x8 slice. The times are simulated.
256 devices in a mesh: head: 8 (over z_lo, core), blk: 32 (over y, x, z_hi).
Axes of the slice: x: 4, y: 4, z: 8 (z_hi: 2, z_lo: 4; z = z_hi * 4 + z_lo), core: 2. Of those that a mesh axis runs over, the one named last changes fastest.
Arguments:
- query_act: bfloat16 [8192, 5120], P(('blk', 'head')), may hold values from -6 to 6
- key_act: bfloat16 [8192, 1024], P(('blk', 'head')), may hold values from -6 to 6
- value_act: bfloat16 [8192, 1024], P(('blk', 'head')), may hold values from -6 to 6
- attn_out: bfloat16 [8192, 5120], P(('blk', 'head')), may hold values from -4 to 4
- grad_out: bfloat16 [8192, 5120], P(('blk', 'head')), may hold values from -6 to 6
- log_sum: float32 [8192, 40], P(('blk', 'head')), may hold values from 5 to 6.5
- kv_lists: int32 [64, 32], P('blk'), may hold values from -1 to 63, as said below
Outputs:
- grad_query: bfloat16 [8192, 5120], P(('blk', 'head'))
- grad_key: bfloat16 [8192, 1024], P(('blk', 'head'))
- grad_value: bfloat16 [8192, 1024], P(('blk', 'head'))
Inputs may be any that keep to these rules, and one draw needn't show every extreme that they name: `kv_lists`: the pack is made of prompt trees: the first holds 16 blocks, the last 16, and those between 32 blocks each, in order. A tree is a prompt, then branches. Row r names in rising order the blocks whose keys block r sees (the tree's prompt blocks up to r, and the earlier blocks of r's branch), then -1 to the end. Every entry lies in the same tree as r and is at most r; r itself is always named.
All inputs are finite; a program needn't handle non-finite values.
Results may differ from a plain program's by a relative error of at most 0.0049.
Values may be sent and summed in bfloat16 or wider, within the bound.
A program may use at most 64 MiB of HBM per device.

v0:
```python
import jax
import jax.numpy as jnp
from jax import lax
from jax.sharding import PartitionSpec as P

QH = 40
KVH = 8
HD = 128
BLOCK = 128


def passed_along(array, axis, by):
    size = lax.axis_size(axis)
    pairs = [(i, i + by) for i in range(size) if 0 <= i + by < size]
    return lax.ppermute(array, axis, pairs)


def shifted(array, axis, by):
    size = lax.axis_size(axis)
    return lax.ppermute(array, axis, [(i, (i + by) % size) for i in range(size)])


def head_delta(grad_rows, out_rows, heads):
    count = grad_rows.shape[0]
    return jnp.einsum(
        "thd,thd->th",
        grad_rows.reshape(count, heads, HD),
        out_rows.reshape(count, heads, HD),
        preferred_element_type=jnp.float32,
    )


def local(query_act, key_act, value_act, attn_out, grad_out, log_sum, kv_lists):
    head_count = lax.axis_size("head")
    blk_count = lax.axis_size("blk")
    query_rows, key_rows, value_rows, grad_rows, total_rows, out_rows = (
        lax.all_to_all(
            query_act.astype(jnp.float32), "head", split_axis=1, concat_axis=0, tiled=True
        ).astype(query_act.dtype),
        lax.all_to_all(
            key_act.astype(jnp.float32), "head", split_axis=1, concat_axis=0, tiled=True
        ).astype(key_act.dtype),
        lax.all_to_all(
            value_act.astype(jnp.float32), "head", split_axis=1, concat_axis=0, tiled=True
        ).astype(value_act.dtype),
        lax.all_to_all(
            grad_out.astype(jnp.float32), "head", split_axis=1, concat_axis=0, tiled=True
        ).astype(grad_out.dtype),
        lax.all_to_all(log_sum, "head", split_axis=1, concat_axis=0, tiled=True),
        lax.all_to_all(
            attn_out.astype(jnp.float32), "head", split_axis=1, concat_axis=0, tiled=True
        ).astype(attn_out.dtype),
    )
    delta_rows = head_delta(grad_rows, out_rows, QH // head_count)
    tokens = query_rows.shape[0]
    local_heads = KVH // head_count
    group_size = QH // KVH
    blocks_dev = tokens // BLOCK
    scaling = HD ** (-0.5)
    queries = query_rows.reshape(tokens, local_heads, group_size, HD)
    out_grads = grad_rows.reshape(tokens, local_heads, group_size, HD)
    row_totals = total_rows.reshape(tokens, local_heads, group_size).transpose(1, 2, 0)[
        :, :, :, None
    ]
    row_deltas = delta_rows.reshape(tokens, local_heads, group_size).transpose(1, 2, 0)[
        :, :, :, None
    ]
    position = lax.axis_index("blk")
    query_pos = position * tokens + jnp.arange(tokens, dtype=jnp.int32)

    def block_mask(rotation):
        source = (position - rotation) % blk_count
        key_ids = source * blocks_dev + jnp.arange(blocks_dev, dtype=jnp.int32)
        listed = jnp.any(kv_lists[:, :, None] == key_ids[None, None, :], axis=1)
        key_pos = source * tokens + jnp.arange(tokens, dtype=jnp.int32)
        return (listed, key_pos)

    def attend(kv_pair, key_sums, query_grad, listed, key_pos):
        visible = jnp.repeat(jnp.repeat(listed, BLOCK, axis=0), BLOCK, axis=1) & (
            key_pos[None, :] <= query_pos[:, None]
        )
        key_block = kv_pair[0].reshape(tokens, local_heads, HD)
        value_block = kv_pair[1].reshape(tokens, local_heads, HD)
        scores = (
            jnp.einsum("tkgd,skd->kgts", queries, key_block, preferred_element_type=jnp.float32)
            * scaling
        )
        weights = jnp.where(visible, jnp.exp(scores - row_totals), 0.0)
        grad_probs = jnp.einsum(
            "tkgd,skd->kgts", out_grads, value_block, preferred_element_type=jnp.float32
        )
        grad_scores = (weights * (grad_probs - row_deltas)).astype(jnp.bfloat16)
        probs_low = weights.astype(jnp.bfloat16)
        value_part = jnp.einsum(
            "kgts,tkgd->skd", probs_low, out_grads, preferred_element_type=jnp.float32
        )
        key_part = (
            jnp.einsum("kgts,tkgd->skd", grad_scores, queries, preferred_element_type=jnp.float32)
            * scaling
        )
        query_part = (
            jnp.einsum("kgts,skd->tkgd", grad_scores, key_block, preferred_element_type=jnp.float32)
            * scaling
        )
        added = jnp.stack(
            [
                key_part.reshape(tokens, local_heads * HD),
                value_part.reshape(tokens, local_heads * HD),
            ]
        )
        return (key_sums + added, query_grad + query_part)

    def visit(rotation, kv_pair, key_sums, query_grad):
        listed, key_pos = block_mask(rotation)
        return attend(kv_pair, key_sums, query_grad, listed, key_pos)

    kv_pair = jnp.stack([key_rows, value_rows])
    empty_sums = jnp.zeros((2, tokens, local_heads * HD), jnp.float32)
    empty_grad = jnp.zeros((tokens, local_heads, group_size, HD), jnp.float32)

    def advance(rotation, carried):
        kv_here, key_sums, query_grad = carried
        arrived = passed_along(kv_here, "blk", 1)
        key_sums, query_grad = visit(rotation, kv_here, key_sums, query_grad)
        key_sums = shifted(key_sums, "blk", 1)
        return (arrived, key_sums, query_grad)

    kv_here, key_sums, query_grad = lax.fori_loop(
        0, blk_count - 1, advance, (kv_pair, empty_sums, empty_grad)
    )
    key_sums, query_grad = visit(blk_count - 1, kv_here, key_sums, query_grad)
    key_sums = shifted(key_sums.astype(jnp.bfloat16), "blk", 1 - blk_count).astype(key_sums.dtype)
    query_low = query_grad.reshape(tokens, local_heads * group_size * HD).astype(jnp.bfloat16)
    key_low = key_sums[0].astype(jnp.bfloat16)
    value_low = key_sums[1].astype(jnp.bfloat16)
    grad_query, grad_key, grad_value = (
        lax.all_to_all(query_low, "head", split_axis=0, concat_axis=1, tiled=True),
        lax.all_to_all(key_low, "head", split_axis=0, concat_axis=1, tiled=True),
        lax.all_to_all(value_low, "head", split_axis=0, concat_axis=1, tiled=True),
    )
    return (grad_query, grad_key, grad_value)


def solution(mesh):
    return jax.shard_map(
        local,
        mesh=mesh,
        in_specs=(
            P(("blk", "head"), None),
            P(("blk", "head"), None),
            P(("blk", "head"), None),
            P(("blk", "head"), None),
            P(("blk", "head"), None),
            P(("blk", "head"), None),
            P("blk", None),
        ),
        out_specs=(P(("blk", "head"), None), P(("blk", "head"), None), P(("blk", "head"), None)),
        check_vma=False,
    )
```

profile of v0, /device:TPU:1, one launch (start us, length us, event | category | flops | bytes accessed | tf_op | source)
XLA Modules:
  0.0 885.4 jit_solution(12147705580826864450)
XLA Ops:
  78.6 715.4 %while.20 = (s32[]{:T(128)}, bf16[2,256,128]{2,1,0:T(8,128)(2,1)S(1)}, f32[2,256,128]{2,1,0:T(8,128)S(1)}, f32[256,1,5,128]{3,0,2,1:T(8,128)S(1)}, s32[2,32]{1,0...) while((s32[]{:T(128)}, ...), condition=%wide.region_2.3_spmd.clone, body=%wide.region_0.2_spmd.clone.sunk | while | flops 422511360 | bytes 11754164 | solution.py:128
  89.5 17.8 %collective-permute-done.1 = f32[2,256,128]{2,1,0:T(8,128)S(1)} collective-permute-done((f32[2,256,128]{2,1,0:T(8,128)S(1)}, f32[2,256,128]{2,1,0:T(8,128)S(1)}, u32[]{:S(2)}, u32[]{:S(2)}) %collective-permute-start.1) | collective-permute-done | bytes 262176 | tf_op jit(solution)/shard_map/while/body/eval_jaxpr/ppermute | solution.py:20
  111.3 15.7 %collective-permute-done.1 = f32[2,256,128]{2,1,0:T(8,128)S(1)} collective-permute-done((f32[2,256,128]{2,1,0:T(8,128)S(1)}, f32[2,256,128]{2,1,0:T(8,128)S(1)}, u32[]{:S(2)}, u32[]{:S(2)}) %collective-permute-start.1) | collective-permute-done | bytes 262176 | tf_op jit(solution)/shard_map/while/body/eval_jaxpr/ppermute | solution.py:20
  132.3 11.8 %collective-permute-done.1 = f32[2,256,128]{2,1,0:T(8,128)S(1)} collective-permute-done((f32[2,256,128]{2,1,0:T(8,128)S(1)}, f32[2,256,128]{2,1,0:T(8,128)S(1)}, u32[]{:S(2)}, u32[]{:S(2)}) %collective-permute-start.1) | collective-permute-done | bytes 262176 | tf_op jit(solution)/shard_map/while/body/eval_jaxpr/ppermute | solution.py:20
  160.9 10.9 %collective-permute-start = (bf16[2,256,128]{2,1,0:T(8,128)(2,1)S(1)}, bf16[2,256,128]{2,1,0:T(8,128)(2,1)S(1)}, u32[]{:S(2)}, u32[]{:S(2)}) collective-permute-start(bf16[2,256,128]{2,1,0:T(8,128)(2,1)S(1)} %copy.135), channel_id=1, source_target_pairs={{0,1},{1,2},{2,3},{3,4},{4,5},{5,6},{6,7},{7,8},{8,9},{9,10},{10,1... | collective-permute-start | bytes 393224 | tf_op jit(solution)/shard_map/while/body/eval_jaxpr/ppermute | solution.py:15
  201.5 13.4 %collective-permute-done.1 = f32[2,256,128]{2,1,0:T(8,128)S(1)} collective-permute-done((f32[2,256,128]{2,1,0:T(8,128)S(1)}, f32[2,256,128]{2,1,0:T(8,128)S(1)}, u32[]{:S(2)}, u32[]{:S(2)}) %collective-permute-start.1) | collective-permute-done | bytes 262176 | tf_op jit(solution)/shard_map/while/body/eval_jaxpr/ppermute | solution.py:20
  219.4 13.7 %collective-permute-done.1 = f32[2,256,128]{2,1,0:T(8,128)S(1)} collective-permute-done((f32[2,256,128]{2,1,0:T(8,128)S(1)}, f32[2,256,128]{2,1,0:T(8,128)S(1)}, u32[]{:S(2)}, u32[]{:S(2)}) %collective-permute-start.1) | collective-permute-done | bytes 262176 | tf_op jit(solution)/shard_map/while/body/eval_jaxpr/ppermute | solution.py:20
  237.8 13.6 %collective-permute-done.1 = f32[2,256,128]{2,1,0:T(8,128)S(1)} collective-permute-done((f32[2,256,128]{2,1,0:T(8,128)S(1)}, f32[2,256,128]{2,1,0:T(8,128)S(1)}, u32[]{:S(2)}, u32[]{:S(2)}) %collective-permute-start.1) | collective-permute-done | bytes 262176 | tf_op jit(solution)/shard_map/while/body/eval_jaxpr/ppermute | solution.py:20
  259.7 17.5 %collective-permute-done.1 = f32[2,256,128]{2,1,0:T(8,128)S(1)} collective-permute-done((f32[2,256,128]{2,1,0:T(8,128)S(1)}, f32[2,256,128]{2,1,0:T(8,128)S(1)}, u32[]{:S(2)}, u32[]{:S(2)}) %collective-permute-start.1) | collective-permute-done | bytes 262176 | tf_op jit(solution)/shard_map/while/body/eval_jaxpr/ppermute | solution.py:20
  285.8 10.4 %collective-permute-done.1 = f32[2,256,128]{2,1,0:T(8,128)S(1)} collective-permute-done((f32[2,256,128]{2,1,0:T(8,128)S(1)}, f32[2,256,128]{2,1,0:T(8,128)S(1)}, u32[]{:S(2)}, u32[]{:S(2)}) %collective-permute-start.1) | collective-permute-done | bytes 262176 | tf_op jit(solution)/shard_map/while/body/eval_jaxpr/ppermute | solution.py:20
  303.1 16.4 %collective-permute-done.1 = f32[2,256,128]{2,1,0:T(8,128)S(1)} collective-permute-done((f32[2,256,128]{2,1,0:T(8,128)S(1)}, f32[2,256,128]{2,1,0:T(8,128)S(1)}, u32[]{:S(2)}, u32[]{:S(2)}) %collective-permute-start.1) | collective-permute-done | bytes 262176 | tf_op jit(solution)/shard_map/while/body/eval_jaxpr/ppermute | solution.py:20
  324.6 11.9 %collective-permute-done.1 = f32[2,256,128]{2,1,0:T(8,128)S(1)} collective-permute-done((f32[2,256,128]{2,1,0:T(8,128)S(1)}, f32[2,256,128]{2,1,0:T(8,128)S(1)}, u32[]{:S(2)}, u32[]{:S(2)}) %collective-permute-start.1) | collective-permute-done | bytes 262176 | tf_op jit(solution)/shard_map/while/body/eval_jaxpr/ppermute | solution.py:20
  359.8 10.7 %collective-permute-start.1 = (f32[2,256,128]{2,1,0:T(8,128)S(1)}, f32[2,256,128]{2,1,0:T(8,128)S(1)}, u32[]{:S(2)}, u32[]{:S(2)}) collective-permute-start(f32[2,256,128]{2,1,0:T(8,128)S(1)} %maximum_add_fusion.3), channel_id=1, source_target_pairs={{0,1},{1,2},{2,3},{3,4},{4,5},{5,6},{6,7},{7,8},{8,9},{9,10},{10,1... | collective-permute-start | bytes 786440 | tf_op jit(solution)/shard_map/while/body/eval_jaxpr/ppermute | solution.py:20
  378.1 12.3 %collective-permute-start = (bf16[2,256,128]{2,1,0:T(8,128)(2,1)S(1)}, bf16[2,256,128]{2,1,0:T(8,128)(2,1)S(1)}, u32[]{:S(2)}, u32[]{:S(2)}) collective-permute-start(bf16[2,256,128]{2,1,0:T(8,128)(2,1)S(1)} %copy.135), channel_id=1, source_target_pairs={{0,1},{1,2},{2,3},{3,4},{4,5},{5,6},{6,7},{7,8},{8,9},{9,10},{10,1... | collective-permute-start | bytes 393224 | tf_op jit(solution)/shard_map/while/body/eval_jaxpr/ppermute | solution.py:15
  400.0 12.3 %collective-permute-done.1 = f32[2,256,128]{2,1,0:T(8,128)S(1)} collective-permute-done((f32[2,256,128]{2,1,0:T(8,128)S(1)}, f32[2,256,128]{2,1,0:T(8,128)S(1)}, u32[]{:S(2)}, u32[]{:S(2)}) %collective-permute-start.1) | collective-permute-done | bytes 262176 | tf_op jit(solution)/shard_map/while/body/eval_jaxpr/ppermute | solution.py:20
  432.5 16.5 %collective-permute-start = (bf16[2,256,128]{2,1,0:T(8,128)(2,1)S(1)}, bf16[2,256,128]{2,1,0:T(8,128)(2,1)S(1)}, u32[]{:S(2)}, u32[]{:S(2)}) collective-permute-start(bf16[2,256,128]{2,1,0:T(8,128)(2,1)S(1)} %copy.135), channel_id=1, source_target_pairs={{0,1},{1,2},{2,3},{3,4},{4,5},{5,6},{6,7},{7,8},{8,9},{9,10},{10,1... | collective-permute-start | bytes 393224 | tf_op jit(solution)/shard_map/while/body/eval_jaxpr/ppermute | solution.py:15
  494.7 10.8 %collective-permute-done.1 = f32[2,256,128]{2,1,0:T(8,128)S(1)} collective-permute-done((f32[2,256,128]{2,1,0:T(8,128)S(1)}, f32[2,256,128]{2,1,0:T(8,128)S(1)}, u32[]{:S(2)}, u32[]{:S(2)}) %collective-permute-start.1) | collective-permute-done | bytes 262176 | tf_op jit(solution)/shard_map/while/body/eval_jaxpr/ppermute | solution.py:20
  530.7 13.6 %collective-permute-start.1 = (f32[2,256,128]{2,1,0:T(8,128)S(1)}, f32[2,256,128]{2,1,0:T(8,128)S(1)}, u32[]{:S(2)}, u32[]{:S(2)}) collective-permute-start(f32[2,256,128]{2,1,0:T(8,128)S(1)} %maximum_add_fusion.3), channel_id=1, source_target_pairs={{0,1},{1,2},{2,3},{3,4},{4,5},{5,6},{6,7},{7,8},{8,9},{9,10},{10,1... | collective-permute-start | bytes 786440 | tf_op jit(solution)/shard_map/while/body/eval_jaxpr/ppermute | solution.py:20
  682.5 10.8 %collective-permute-done.1 = f32[2,256,128]{2,1,0:T(8,128)S(1)} collective-permute-done((f32[2,256,128]{2,1,0:T(8,128)S(1)}, f32[2,256,128]{2,1,0:T(8,128)S(1)}, u32[]{:S(2)}, u32[]{:S(2)}) %collective-permute-start.1) | collective-permute-done | bytes 262176 | tf_op jit(solution)/shard_map/while/body/eval_jaxpr/ppermute | solution.py:20
  702.9 12.1 %collective-permute-done.1 = f32[2,256,128]{2,1,0:T(8,128)S(1)} collective-permute-done((f32[2,256,128]{2,1,0:T(8,128)S(1)}, f32[2,256,128]{2,1,0:T(8,128)S(1)}, u32[]{:S(2)}, u32[]{:S(2)}) %collective-permute-start.1) | collective-permute-done | bytes 262176 | tf_op jit(solution)/shard_map/while/body/eval_jaxpr/ppermute | solution.py:20
  728.5 15.6 %collective-permute-done.1 = f32[2,256,128]{2,1,0:T(8,128)S(1)} collective-permute-done((f32[2,256,128]{2,1,0:T(8,128)S(1)}, f32[2,256,128]{2,1,0:T(8,128)S(1)}, u32[]{:S(2)}, u32[]{:S(2)}) %collective-permute-start.1) | collective-permute-done | bytes 262176 | tf_op jit(solution)/shard_map/while/body/eval_jaxpr/ppermute | solution.py:20
  777.3 16.6 %collective-permute-done.1 = f32[2,256,128]{2,1,0:T(8,128)S(1)} collective-permute-done((f32[2,256,128]{2,1,0:T(8,128)S(1)}, f32[2,256,128]{2,1,0:T(8,128)S(1)}, u32[]{:S(2)}, u32[]{:S(2)}) %collective-permute-start.1) | collective-permute-done | bytes 262176 | tf_op jit(solution)/shard_map/while/body/eval_jaxpr/ppermute | solution.py:20
  797.3 13.5 %collective-permute-done.2 = bf16[2,256,128]{2,1,0:T(8,128)(2,1)S(1)} collective-permute-done((bf16[2,256,128]{2,1,0:T(8,128)(2,1)S(1)}, bf16[2,256,128]{2,1,0:T(8,128)(2,1)S(1)}, u32[]{:S(2)}, u32[]{:S(2)}) %collective-permute-start.2) | collective-permute-done | bytes 131104 | tf_op jit(solution)/shard_map/ppermute | solution.py:20
  811.4 44.8 %all-to-all-start.7 = ((bf16[8,32,128]{2,1,0:T(8,128)(2,1)}), bf16[8,32,128]{2,1,0:T(8,128)(2,1)S(1)}, u32[]{:S(2)}, u32[]{:S(2)}) async-start(bf16[8,32,128]{2,1,0:T(8,128)(2,1)} %bitcast.41), calls=%async_computation.7 | async-start | bytes 131072 | tf_op jit(solution)/shard_map/all_to_all | solution.py:138
  (642 shorter events, 538.1 us)
Async XLA Ops:
  86.9 20.5 %collective-permute-start.1 = (f32[2,256,128]{2,1,0:T(8,128)S(1)}, f32[2,256,128]{2,1,0:T(8,128)S(1)}, u32[]{:S(2)}, u32[]{:S(2)}) collective-permute-start(f32[2,256,128]{2,1,0:T(8,128)S(1)} %maximum_add_fusion.3), channel_id=1, source_target_pairs={{0,1},{1,2},{2,3},{3,4},{4,5},{5,6},{6,7},{7,8},{8,9},{9,10},{10,1... | collective-permute-start | bytes 786440 | tf_op jit(solution)/shard_map/while/body/eval_jaxpr/ppermute | solution.py:20
  110.7 16.3 %collective-permute-start.1 = (f32[2,256,128]{2,1,0:T(8,128)S(1)}, f32[2,256,128]{2,1,0:T(8,128)S(1)}, u32[]{:S(2)}, u32[]{:S(2)}) collective-permute-start(f32[2,256,128]{2,1,0:T(8,128)S(1)} %maximum_add_fusion.3), channel_id=1, source_target_pairs={{0,1},{1,2},{2,3},{3,4},{4,5},{5,6},{6,7},{7,8},{8,9},{9,10},{10,1... | collective-permute-start | bytes 786440 | tf_op jit(solution)/shard_map/while/body/eval_jaxpr/ppermute | solution.py:20
  160.9 20.7 %collective-permute-start = (bf16[2,256,128]{2,1,0:T(8,128)(2,1)S(1)}, bf16[2,256,128]{2,1,0:T(8,128)(2,1)S(1)}, u32[]{:S(2)}, u32[]{:S(2)}) collective-permute-start(bf16[2,256,128]{2,1,0:T(8,128)(2,1)S(1)} %copy.135), channel_id=1, source_target_pairs={{0,1},{1,2},{2,3},{3,4},{4,5},{5,6},{6,7},{7,8},{8,9},{9,10},{10,1... | collective-permute-start | bytes 393224 | tf_op jit(solution)/shard_map/while/body/eval_jaxpr/ppermute | solution.py:15
  196.8 18.1 %collective-permute-start.1 = (f32[2,256,128]{2,1,0:T(8,128)S(1)}, f32[2,256,128]{2,1,0:T(8,128)S(1)}, u32[]{:S(2)}, u32[]{:S(2)}) collective-permute-start(f32[2,256,128]{2,1,0:T(8,128)S(1)} %maximum_add_fusion.3), channel_id=1, source_target_pairs={{0,1},{1,2},{2,3},{3,4},{4,5},{5,6},{6,7},{7,8},{8,9},{9,10},{10,1... | collective-permute-start | bytes 786440 | tf_op jit(solution)/shard_map/while/body/eval_jaxpr/ppermute | solution.py:20
  254.7 22.4 %collective-permute-start.1 = (f32[2,256,128]{2,1,0:T(8,128)S(1)}, f32[2,256,128]{2,1,0:T(8,128)S(1)}, u32[]{:S(2)}, u32[]{:S(2)}) collective-permute-start(f32[2,256,128]{2,1,0:T(8,128)S(1)} %maximum_add_fusion.3), channel_id=1, source_target_pairs={{0,1},{1,2},{2,3},{3,4},{4,5},{5,6},{6,7},{7,8},{8,9},{9,10},{10,1... | collective-permute-start | bytes 786440 | tf_op jit(solution)/shard_map/while/body/eval_jaxpr/ppermute | solution.py:20
  301.5 18.1 %collective-permute-start.1 = (f32[2,256,128]{2,1,0:T(8,128)S(1)}, f32[2,256,128]{2,1,0:T(8,128)S(1)}, u32[]{:S(2)}, u32[]{:S(2)}) collective-permute-start(f32[2,256,128]{2,1,0:T(8,128)S(1)} %maximum_add_fusion.3), channel_id=1, source_target_pairs={{0,1},{1,2},{2,3},{3,4},{4,5},{5,6},{6,7},{7,8},{8,9},{9,10},{10,1... | collective-permute-start | bytes 786440 | tf_op jit(solution)/shard_map/while/body/eval_jaxpr/ppermute | solution.py:20
  359.8 18.3 %collective-permute-start.1 = (f32[2,256,128]{2,1,0:T(8,128)S(1)}, f32[2,256,128]{2,1,0:T(8,128)S(1)}, u32[]{:S(2)}, u32[]{:S(2)}) collective-permute-start(f32[2,256,128]{2,1,0:T(8,128)S(1)} %maximum_add_fusion.3), channel_id=1, source_target_pairs={{0,1},{1,2},{2,3},{3,4},{4,5},{5,6},{6,7},{7,8},{8,9},{9,10},{10,1... | collective-permute-start | bytes 786440 | tf_op jit(solution)/shard_map/while/body/eval_jaxpr/ppermute | solution.py:20
  378.1 21.9 %collective-permute-start = (bf16[2,256,128]{2,1,0:T(8,128)(2,1)S(1)}, bf16[2,256,128]{2,1,0:T(8,128)(2,1)S(1)}, u32[]{:S(2)}, u32[]{:S(2)}) collective-permute-start(bf16[2,256,128]{2,1,0:T(8,128)(2,1)S(1)} %copy.135), channel_id=1, source_target_pairs={{0,1},{1,2},{2,3},{3,4},{4,5},{5,6},{6,7},{7,8},{8,9},{9,10},{10,1... | collective-permute-start | bytes 393224 | tf_op jit(solution)/shard_map/while/body/eval_jaxpr/ppermute | solution.py:15
  392.4 19.9 %collective-permute-start.1 = (f32[2,256,128]{2,1,0:T(8,128)S(1)}, f32[2,256,128]{2,1,0:T(8,128)S(1)}, u32[]{:S(2)}, u32[]{:S(2)}) collective-permute-start(f32[2,256,128]{2,1,0:T(8,128)S(1)} %maximum_add_fusion.3), channel_id=1, source_target_pairs={{0,1},{1,2},{2,3},{3,4},{4,5},{5,6},{6,7},{7,8},{8,9},{9,10},{10,1... | collective-permute-start | bytes 786440 | tf_op jit(solution)/shard_map/while/body/eval_jaxpr/ppermute | solution.py:20
  432.5 26.2 %collective-permute-start = (bf16[2,256,128]{2,1,0:T(8,128)(2,1)S(1)}, bf16[2,256,128]{2,1,0:T(8,128)(2,1)S(1)}, u32[]{:S(2)}, u32[]{:S(2)}) collective-permute-start(bf16[2,256,128]{2,1,0:T(8,128)(2,1)S(1)} %copy.135), channel_id=1, source_target_pairs={{0,1},{1,2},{2,3},{3,4},{4,5},{5,6},{6,7},{7,8},{8,9},{9,10},{10,1... | collective-permute-start | bytes 393224 | tf_op jit(solution)/shard_map/while/body/eval_jaxpr/ppermute | solution.py:15
  451.0 17.8 %collective-permute-start.1 = (f32[2,256,128]{2,1,0:T(8,128)S(1)}, f32[2,256,128]{2,1,0:T(8,128)S(1)}, u32[]{:S(2)}, u32[]{:S(2)}) collective-permute-start(f32[2,256,128]{2,1,0:T(8,128)S(1)} %maximum_add_fusion.3), channel_id=1, source_target_pairs={{0,1},{1,2},{2,3},{3,4},{4,5},{5,6},{6,7},{7,8},{8,9},{9,10},{10,1... | collective-permute-start | bytes 786440 | tf_op jit(solution)/shard_map/while/body/eval_jaxpr/ppermute | solution.py:20
  489.7 15.8 %collective-permute-start.1 = (f32[2,256,128]{2,1,0:T(8,128)S(1)}, f32[2,256,128]{2,1,0:T(8,128)S(1)}, u32[]{:S(2)}, u32[]{:S(2)}) collective-permute-start(f32[2,256,128]{2,1,0:T(8,128)S(1)} %maximum_add_fusion.3), channel_id=1, source_target_pairs={{0,1},{1,2},{2,3},{3,4},{4,5},{5,6},{6,7},{7,8},{8,9},{9,10},{10,1... | collective-permute-start | bytes 786440 | tf_op jit(solution)/shard_map/while/body/eval_jaxpr/ppermute | solution.py:20
  523.8 21.0 %collective-permute-start = (bf16[2,256,128]{2,1,0:T(8,128)(2,1)S(1)}, bf16[2,256,128]{2,1,0:T(8,128)(2,1)S(1)}, u32[]{:S(2)}, u32[]{:S(2)}) collective-permute-start(bf16[2,256,128]{2,1,0:T(8,128)(2,1)S(1)} %copy.135), channel_id=1, source_target_pairs={{0,1},{1,2},{2,3},{3,4},{4,5},{5,6},{6,7},{7,8},{8,9},{9,10},{10,1... | collective-permute-start | bytes 393224 | tf_op jit(solution)/shard_map/while/body/eval_jaxpr/ppermute | solution.py:15
  530.7 17.4 %collective-permute-start.1 = (f32[2,256,128]{2,1,0:T(8,128)S(1)}, f32[2,256,128]{2,1,0:T(8,128)S(1)}, u32[]{:S(2)}, u32[]{:S(2)}) collective-permute-start(f32[2,256,128]{2,1,0:T(8,128)S(1)} %maximum_add_fusion.3), channel_id=1, source_target_pairs={{0,1},{1,2},{2,3},{3,4},{4,5},{5,6},{6,7},{7,8},{8,9},{9,10},{10,1... | collective-permute-start | bytes 786440 | tf_op jit(solution)/shard_map/while/body/eval_jaxpr/ppermute | solution.py:20
  548.1 19.4 %collective-permute-start = (bf16[2,256,128]{2,1,0:T(8,128)(2,1)S(1)}, bf16[2,256,128]{2,1,0:T(8,128)(2,1)S(1)}, u32[]{:S(2)}, u32[]{:S(2)}) collective-permute-start(bf16[2,256,128]{2,1,0:T(8,128)(2,1)S(1)} %copy.135), channel_id=1, source_target_pairs={{0,1},{1,2},{2,3},{3,4},{4,5},{5,6},{6,7},{7,8},{8,9},{9,10},{10,1... | collective-permute-start | bytes 393224 | tf_op jit(solution)/shard_map/while/body/eval_jaxpr/ppermute | solution.py:15
  560.2 16.3 %collective-permute-start.1 = (f32[2,256,128]{2,1,0:T(8,128)S(1)}, f32[2,256,128]{2,1,0:T(8,128)S(1)}, u32[]{:S(2)}, u32[]{:S(2)}) collective-permute-start(f32[2,256,128]{2,1,0:T(8,128)S(1)} %maximum_add_fusion.3), channel_id=1, source_target_pairs={{0,1},{1,2},{2,3},{3,4},{4,5},{5,6},{6,7},{7,8},{8,9},{9,10},{10,1... | collective-permute-start | bytes 786440 | tf_op jit(solution)/shard_map/while/body/eval_jaxpr/ppermute | solution.py:20
  581.3 16.5 %collective-permute-start.1 = (f32[2,256,128]{2,1,0:T(8,128)S(1)}, f32[2,256,128]{2,1,0:T(8,128)S(1)}, u32[]{:S(2)}, u32[]{:S(2)}) collective-permute-start(f32[2,256,128]{2,1,0:T(8,128)S(1)} %maximum_add_fusion.3), channel_id=1, source_target_pairs={{0,1},{1,2},{2,3},{3,4},{4,5},{5,6},{6,7},{7,8},{8,9},{9,10},{10,1... | collective-permute-start | bytes 786440 | tf_op jit(solution)/shard_map/while/body/eval_jaxpr/ppermute | solution.py:20
  597.8 17.1 %collective-permute-start = (bf16[2,256,128]{2,1,0:T(8,128)(2,1)S(1)}, bf16[2,256,128]{2,1,0:T(8,128)(2,1)S(1)}, u32[]{:S(2)}, u32[]{:S(2)}) collective-permute-start(bf16[2,256,128]{2,1,0:T(8,128)(2,1)S(1)} %copy.135), channel_id=1, source_target_pairs={{0,1},{1,2},{2,3},{3,4},{4,5},{5,6},{6,7},{7,8},{8,9},{9,10},{10,1... | collective-permute-start | bytes 393224 | tf_op jit(solution)/shard_map/while/body/eval_jaxpr/ppermute | solution.py:15
  623.1 17.0 %collective-permute-start = (bf16[2,256,128]{2,1,0:T(8,128)(2,1)S(1)}, bf16[2,256,128]{2,1,0:T(8,128)(2,1)S(1)}, u32[]{:S(2)}, u32[]{:S(2)}) collective-permute-start(bf16[2,256,128]{2,1,0:T(8,128)(2,1)S(1)} %copy.135), channel_id=1, source_target_pairs={{0,1},{1,2},{2,3},{3,4},{4,5},{5,6},{6,7},{7,8},{8,9},{9,10},{10,1... | collective-permute-start | bytes 393224 | tf_op jit(solution)/shard_map/while/body/eval_jaxpr/ppermute | solution.py:15
  645.1 17.3 %collective-permute-start = (bf16[2,256,128]{2,1,0:T(8,128)(2,1)S(1)}, bf16[2,256,128]{2,1,0:T(8,128)(2,1)S(1)}, u32[]{:S(2)}, u32[]{:S(2)}) collective-permute-start(bf16[2,256,128]{2,1,0:T(8,128)(2,1)S(1)} %copy.135), channel_id=1, source_target_pairs={{0,1},{1,2},{2,3},{3,4},{4,5},{5,6},{6,7},{7,8},{8,9},{9,10},{10,1... | collective-permute-start | bytes 393224 | tf_op jit(solution)/shard_map/while/body/eval_jaxpr/ppermute | solution.py:15
  697.5 17.5 %collective-permute-start.1 = (f32[2,256,128]{2,1,0:T(8,128)S(1)}, f32[2,256,128]{2,1,0:T(8,128)S(1)}, u32[]{:S(2)}, u32[]{:S(2)}) collective-permute-start(f32[2,256,128]{2,1,0:T(8,128)S(1)} %maximum_add_fusion.3), channel_id=1, source_target_pairs={{0,1},{1,2},{2,3},{3,4},{4,5},{5,6},{6,7},{7,8},{8,9},{9,10},{10,1... | collective-permute-start | bytes 786440 | tf_op jit(solution)/shard_map/while/body/eval_jaxpr/ppermute | solution.py:20
  724.5 19.5 %collective-permute-start.1 = (f32[2,256,128]{2,1,0:T(8,128)S(1)}, f32[2,256,128]{2,1,0:T(8,128)S(1)}, u32[]{:S(2)}, u32[]{:S(2)}) collective-permute-start(f32[2,256,128]{2,1,0:T(8,128)S(1)} %maximum_add_fusion.3), channel_id=1, source_target_pairs={{0,1},{1,2},{2,3},{3,4},{4,5},{5,6},{6,7},{7,8},{8,9},{9,10},{10,1... | collective-permute-start | bytes 786440 | tf_op jit(solution)/shard_map/while/body/eval_jaxpr/ppermute | solution.py:20
  773.1 20.8 %collective-permute-start.1 = (f32[2,256,128]{2,1,0:T(8,128)S(1)}, f32[2,256,128]{2,1,0:T(8,128)S(1)}, u32[]{:S(2)}, u32[]{:S(2)}) collective-permute-start(f32[2,256,128]{2,1,0:T(8,128)S(1)} %maximum_add_fusion.3), channel_id=1, source_target_pairs={{0,1},{1,2},{2,3},{3,4},{4,5},{5,6},{6,7},{7,8},{8,9},{9,10},{10,1... | collective-permute-start | bytes 786440 | tf_op jit(solution)/shard_map/while/body/eval_jaxpr/ppermute | solution.py:20
  811.4 49.8 %all-to-all-start.7 = ((bf16[8,32,128]{2,1,0:T(8,128)(2,1)}), bf16[8,32,128]{2,1,0:T(8,128)(2,1)S(1)}, u32[]{:S(2)}, u32[]{:S(2)}) async-start(bf16[8,32,128]{2,1,0:T(8,128)(2,1)} %bitcast.41), calls=%async_computation.7 | async-start | bytes 131072 | tf_op jit(solution)/shard_map/all_to_all | solution.py:138
  (53 other events, 652.3 us)
where the time goes:
time: 887 us; the launch traced here: 885 us
  waiting for transfers between devices  413 us (47%)
  starting transfers between devices  370 us (42%)
  matrix products  62.8 us (7%)
  local copies, waits for them, and re-layouts  23 us (3%)
  other arithmetic  11.9 us (1%)
    ppermute x32, waiting for transfers between devices, shifted(): lax.ppermute(array, axis, [(i, (i + by) % size) for i in range(size)])  351 us
    ppermute x32, starting transfers between devices, shifted(): lax.ppermute(array, axis, [(i, (i + by) % size) for i in range(size)])  146 us
    ppermute x31, starting transfers between devices, passed_along(): return lax.ppermute(array, axis, pairs)  142 us
    all_to_all x1, starting transfers between devices, local(): lax.all_to_all(key_low, 'head', split_axis=0, concat_axis=1, tiled=True)  44.8 us
  transfers between devices with their start and end apart: 72, of which 46 were waited for; matrix products, arithmetic and copies ran while one was open for 10% of the time, Pallas kernels for 0%

commit v1 on v0

--- a/solution.py
+++ b/solution.py
@@ -135,7 +135,12 @@
     value_low = key_sums[1].astype(jnp.bfloat16)
     grad_query, grad_key, grad_value = (
         lax.all_to_all(query_low, "head", split_axis=0, concat_axis=1, tiled=True),
-        lax.all_to_all(key_low, "head", split_axis=0, concat_axis=1, tiled=True),
+        jnp.concatenate(
+            lax.all_to_all(
+                jnp.stack(jnp.split(key_low, lax.axis_size("head"), axis=0)), "head", 0, 0
+            ),
+            axis=1,
+        ),
         lax.all_to_all(value_low, "head", split_axis=0, concat_axis=1, tiled=True),
     )
     return (grad_query, grad_key, grad_value)

time: 887 us -> 893 us (level)
  the two profiles are of different devices: /device:TPU:1 before, /device:TPU:16 now
where the time goes in v1:
time: 893 us; the launch traced here: 891 us
  waiting for transfers between devices  491 us (55%)
  starting transfers between devices  292 us (33%)
  matrix products  62.8 us (7%)
  local copies, waits for them, and re-layouts  27.9 us (3%)
  other arithmetic  12 us (1%)
    ppermute x32, waiting for transfers between devices, shifted(): lax.ppermute(array, axis, [(i, (i + by) % size) for i in range(size)])  244 us
    ppermute x31, waiting for transfers between devices, passed_along(): return lax.ppermute(array, axis, pairs)  187 us
    ppermute x31, starting transfers between devices, passed_along(): return lax.ppermute(array, axis, pairs)  134 us
    ppermute x32, starting transfers between devices, shifted(): lax.ppermute(array, axis, [(i, (i + by) % size) for i in range(size)])  120 us
  transfers between devices with their start and end apart: 72, of which 64 were waited for; matrix products, arithmetic and copies ran while one was open for 10% of the time, Pallas kernels for 0%

profile of v1, /device:TPU:16, one launch (start us, length us, event | category | flops | bytes accessed | tf_op | source)
XLA Modules:
  0.0 891.0 jit_solution(14437104499211950324)
XLA Ops:
  36.5 10.3 %all-to-all-done.2 = bf16[32,8,640]{2,0,1:T(8,128)(2,1)S(1)} async-done(((bf16[32,8,640]{2,0,1:T(8,128)(2,1)}), bf16[32,8,640]{2,0,1:T(8,128)(2,1)S(1)}, u32[]{:S(2)}, u32[]{:S(2)}) %all-to-all-start.2) | async-done | bytes 327712 | tf_op jit(solution)/shard_map/all_to_all | solution.py:37
  51.3 9.9 %all-to-all-done.4 = bf16[32,8,640]{2,0,1:T(8,128)(2,1)S(1)} async-done(((bf16[32,8,640]{2,0,1:T(8,128)(2,1)}), bf16[32,8,640]{2,0,1:T(8,128)(2,1)S(1)}, u32[]{:S(2)}, u32[]{:S(2)}) %all-to-all-start.4) | async-done | bytes 327712 | tf_op jit(solution)/shard_map/all_to_all | solution.py:46
  78.2 755.3 %while.20 = (s32[]{:T(128)}, bf16[2,256,128]{2,1,0:T(8,128)(2,1)S(1)}, f32[2,256,128]{2,1,0:T(8,128)S(1)}, f32[256,1,5,128]{3,0,2,1:T(8,128)S(1)}, s32[2,32]{1,0...) while((s32[]{:T(128)}, ...), condition=%wide.region_2.3_spmd.clone, body=%wide.region_0.2_spmd.clone.sunk | while | flops 422511360 | bytes 11754164 | solution.py:128
  185.1 11.2 %collective-permute-done.1 = f32[2,256,128]{2,1,0:T(8,128)S(1)} collective-permute-done((f32[2,256,128]{2,1,0:T(8,128)S(1)}, f32[2,256,128]{2,1,0:T(8,128)S(1)}, u32[]{:S(2)}, u32[]{:S(2)}) %collective-permute-start.1) | collective-permute-done | bytes 262176 | tf_op jit(solution)/shard_map/while/body/eval_jaxpr/ppermute | solution.py:20
  213.1 13.4 %collective-permute-done.1 = f32[2,256,128]{2,1,0:T(8,128)S(1)} collective-permute-done((f32[2,256,128]{2,1,0:T(8,128)S(1)}, f32[2,256,128]{2,1,0:T(8,128)S(1)}, u32[]{:S(2)}, u32[]{:S(2)}) %collective-permute-start.1) | collective-permute-done | bytes 262176 | tf_op jit(solution)/shard_map/while/body/eval_jaxpr/ppermute | solution.py:20
  235.3 11.9 %collective-permute-done = bf16[2,256,128]{2,1,0:T(8,128)(2,1)S(1)} collective-permute-done((bf16[2,256,128]{2,1,0:T(8,128)(2,1)S(1)}, bf16[2,256,128]{2,1,0:T(8,128)(2,1)S(1)}, u32[]{:S(2)}, u32[]{:S(2)}) %collective-permute-start) | collective-permute-done | bytes 131104 | tf_op jit(solution)/shard_map/while/body/eval_jaxpr/ppermute | solution.py:15
  256.0 14.4 %collective-permute-done = bf16[2,256,128]{2,1,0:T(8,128)(2,1)S(1)} collective-permute-done((bf16[2,256,128]{2,1,0:T(8,128)(2,1)S(1)}, bf16[2,256,128]{2,1,0:T(8,128)(2,1)S(1)}, u32[]{:S(2)}, u32[]{:S(2)}) %collective-permute-start) | collective-permute-done | bytes 131104 | tf_op jit(solution)/shard_map/while/body/eval_jaxpr/ppermute | solution.py:15
  280.9 13.5 %collective-permute-done = bf16[2,256,128]{2,1,0:T(8,128)(2,1)S(1)} collective-permute-done((bf16[2,256,128]{2,1,0:T(8,128)(2,1)S(1)}, bf16[2,256,128]{2,1,0:T(8,128)(2,1)S(1)}, u32[]{:S(2)}, u32[]{:S(2)}) %collective-permute-start) | collective-permute-done | bytes 131104 | tf_op jit(solution)/shard_map/while/body/eval_jaxpr/ppermute | solution.py:15
  305.4 12.9 %collective-permute-done = bf16[2,256,128]{2,1,0:T(8,128)(2,1)S(1)} collective-permute-done((bf16[2,256,128]{2,1,0:T(8,128)(2,1)S(1)}, bf16[2,256,128]{2,1,0:T(8,128)(2,1)S(1)}, u32[]{:S(2)}, u32[]{:S(2)}) %collective-permute-start) | collective-permute-done | bytes 131104 | tf_op jit(solution)/shard_map/while/body/eval_jaxpr/ppermute | solution.py:15
  329.0 13.0 %collective-permute-done = bf16[2,256,128]{2,1,0:T(8,128)(2,1)S(1)} collective-permute-done((bf16[2,256,128]{2,1,0:T(8,128)(2,1)S(1)}, bf16[2,256,128]{2,1,0:T(8,128)(2,1)S(1)}, u32[]{:S(2)}, u32[]{:S(2)}) %collective-permute-start) | collective-permute-done | bytes 131104 | tf_op jit(solution)/shard_map/while/body/eval_jaxpr/ppermute | solution.py:15
  354.1 13.8 %collective-permute-done = bf16[2,256,128]{2,1,0:T(8,128)(2,1)S(1)} collective-permute-done((bf16[2,256,128]{2,1,0:T(8,128)(2,1)S(1)}, bf16[2,256,128]{2,1,0:T(8,128)(2,1)S(1)}, u32[]{:S(2)}, u32[]{:S(2)}) %collective-permute-start) | collective-permute-done | bytes 131104 | tf_op jit(solution)/shard_map/while/body/eval_jaxpr/ppermute | solution.py:15
  523.2 9.6 %collective-permute-done.1 = f32[2,256,128]{2,1,0:T(8,128)S(1)} collective-permute-done((f32[2,256,128]{2,1,0:T(8,128)S(1)}, f32[2,256,128]{2,1,0:T(8,128)S(1)}, u32[]{:S(2)}, u32[]{:S(2)}) %collective-permute-start.1) | collective-permute-done | bytes 262176 | tf_op jit(solution)/shard_map/while/body/eval_jaxpr/ppermute | solution.py:20
  543.2 11.4 %collective-permute-start.1 = (f32[2,256,128]{2,1,0:T(8,128)S(1)}, f32[2,256,128]{2,1,0:T(8,128)S(1)}, u32[]{:S(2)}, u32[]{:S(2)}) collective-permute-start(f32[2,256,128]{2,1,0:T(8,128)S(1)} %maximum_add_fusion.3), channel_id=1, source_target_pairs={{0,1},{1,2},{2,3},{3,4},{4,5},{5,6},{6,7},{7,8},{8,9},{9,10},{10,1... | collective-permute-start | bytes 786440 | tf_op jit(solution)/shard_map/while/body/eval_jaxpr/ppermute | solution.py:20
  555.1 9.7 %collective-permute-done.1 = f32[2,256,128]{2,1,0:T(8,128)S(1)} collective-permute-done((f32[2,256,128]{2,1,0:T(8,128)S(1)}, f32[2,256,128]{2,1,0:T(8,128)S(1)}, u32[]{:S(2)}, u32[]{:S(2)}) %collective-permute-start.1) | collective-permute-done | bytes 262176 | tf_op jit(solution)/shard_map/while/body/eval_jaxpr/ppermute | solution.py:20
  579.0 12.8 %collective-permute-done.1 = f32[2,256,128]{2,1,0:T(8,128)S(1)} collective-permute-done((f32[2,256,128]{2,1,0:T(8,128)S(1)}, f32[2,256,128]{2,1,0:T(8,128)S(1)}, u32[]{:S(2)}, u32[]{:S(2)}) %collective-permute-start.1) | collective-permute-done | bytes 262176 | tf_op jit(solution)/shard_map/while/body/eval_jaxpr/ppermute | solution.py:20
  633.8 9.3 %collective-permute-done.1 = f32[2,256,128]{2,1,0:T(8,128)S(1)} collective-permute-done((f32[2,256,128]{2,1,0:T(8,128)S(1)}, f32[2,256,128]{2,1,0:T(8,128)S(1)}, u32[]{:S(2)}, u32[]{:S(2)}) %collective-permute-start.1) | collective-permute-done | bytes 262176 | tf_op jit(solution)/shard_map/while/body/eval_jaxpr/ppermute | solution.py:20
  657.0 9.8 %collective-permute-done.1 = f32[2,256,128]{2,1,0:T(8,128)S(1)} collective-permute-done((f32[2,256,128]{2,1,0:T(8,128)S(1)}, f32[2,256,128]{2,1,0:T(8,128)S(1)}, u32[]{:S(2)}, u32[]{:S(2)}) %collective-permute-start.1) | collective-permute-done | bytes 262176 | tf_op jit(solution)/shard_map/while/body/eval_jaxpr/ppermute | solution.py:20
  704.7 16.5 %collective-permute-done.1 = f32[2,256,128]{2,1,0:T(8,128)S(1)} collective-permute-done((f32[2,256,128]{2,1,0:T(8,128)S(1)}, f32[2,256,128]{2,1,0:T(8,128)S(1)}, u32[]{:S(2)}, u32[]{:S(2)}) %collective-permute-start.1) | collective-permute-done | bytes 262176 | tf_op jit(solution)/shard_map/while/body/eval_jaxpr/ppermute | solution.py:20
  747.4 10.7 %collective-permute-done = bf16[2,256,128]{2,1,0:T(8,128)(2,1)S(1)} collective-permute-done((bf16[2,256,128]{2,1,0:T(8,128)(2,1)S(1)}, bf16[2,256,128]{2,1,0:T(8,128)(2,1)S(1)}, u32[]{:S(2)}, u32[]{:S(2)}) %collective-permute-start) | collective-permute-done | bytes 131104 | tf_op jit(solution)/shard_map/while/body/eval_jaxpr/ppermute | solution.py:15
  765.5 14.0 %collective-permute-done = bf16[2,256,128]{2,1,0:T(8,128)(2,1)S(1)} collective-permute-done((bf16[2,256,128]{2,1,0:T(8,128)(2,1)S(1)}, bf16[2,256,128]{2,1,0:T(8,128)(2,1)S(1)}, u32[]{:S(2)}, u32[]{:S(2)}) %collective-permute-start) | collective-permute-done | bytes 131104 | tf_op jit(solution)/shard_map/while/body/eval_jaxpr/ppermute | solution.py:15
  792.8 11.0 %collective-permute-done = bf16[2,256,128]{2,1,0:T(8,128)(2,1)S(1)} collective-permute-done((bf16[2,256,128]{2,1,0:T(8,128)(2,1)S(1)}, bf16[2,256,128]{2,1,0:T(8,128)(2,1)S(1)}, u32[]{:S(2)}, u32[]{:S(2)}) %collective-permute-start) | collective-permute-done | bytes 131104 | tf_op jit(solution)/shard_map/while/body/eval_jaxpr/ppermute | solution.py:15
  814.8 12.5 %collective-permute-done = bf16[2,256,128]{2,1,0:T(8,128)(2,1)S(1)} collective-permute-done((bf16[2,256,128]{2,1,0:T(8,128)(2,1)S(1)}, bf16[2,256,128]{2,1,0:T(8,128)(2,1)S(1)}, u32[]{:S(2)}, u32[]{:S(2)}) %collective-permute-start) | collective-permute-done | bytes 131104 | tf_op jit(solution)/shard_map/while/body/eval_jaxpr/ppermute | solution.py:15
  836.8 11.9 %collective-permute-done.2 = bf16[2,256,128]{2,1,0:T(8,128)(2,1)S(1)} collective-permute-done((bf16[2,256,128]{2,1,0:T(8,128)(2,1)S(1)}, bf16[2,256,128]{2,1,0:T(8,128)(2,1)S(1)}, u32[]{:S(2)}, u32[]{:S(2)}) %collective-permute-start.2) | collective-permute-done | bytes 131104 | tf_op jit(solution)/shard_map/ppermute | solution.py:20
  880.5 9.8 %all-to-all-done.6 = bf16[8,32,640]{2,1,0:T(8,128)(2,1)S(1)} async-done(((bf16[8,32,640]{2,1,0:T(8,128)(2,1)}), bf16[8,32,640]{2,1,0:T(8,128)(2,1)S(1)}, u32[]{:S(2)}, u32[]{:S(2)}) %all-to-all-start.6) | async-done | bytes 327712 | tf_op jit(solution)/shard_map/all_to_all | solution.py:137
  (650 shorter events, 612.8 us)
Async XLA Ops:
  78.3 17.7 %collective-permute-start = (bf16[2,256,128]{2,1,0:T(8,128)(2,1)S(1)}, bf16[2,256,128]{2,1,0:T(8,128)(2,1)S(1)}, u32[]{:S(2)}, u32[]{:S(2)}) collective-permute-start(bf16[2,256,128]{2,1,0:T(8,128)(2,1)S(1)} %copy.134), channel_id=1, source_target_pairs={{0,1},{1,2},{2,3},{3,4},{4,5},{5,6},{6,7},{7,8},{8,9},{9,10},{10,1... | collective-permute-start | bytes 393224 | tf_op jit(solution)/shard_map/while/body/eval_jaxpr/ppermute | solution.py:15
  176.0 20.3 %collective-permute-start.1 = (f32[2,256,128]{2,1,0:T(8,128)S(1)}, f32[2,256,128]{2,1,0:T(8,128)S(1)}, u32[]{:S(2)}, u32[]{:S(2)}) collective-permute-start(f32[2,256,128]{2,1,0:T(8,128)S(1)} %maximum_add_fusion.3), channel_id=1, source_target_pairs={{0,1},{1,2},{2,3},{3,4},{4,5},{5,6},{6,7},{7,8},{8,9},{9,10},{10,1... | collective-permute-start | bytes 786440 | tf_op jit(solution)/shard_map/while/body/eval_jaxpr/ppermute | solution.py:20
  206.7 19.8 %collective-permute-start.1 = (f32[2,256,128]{2,1,0:T(8,128)S(1)}, f32[2,256,128]{2,1,0:T(8,128)S(1)}, u32[]{:S(2)}, u32[]{:S(2)}) collective-permute-start(f32[2,256,128]{2,1,0:T(8,128)S(1)} %maximum_add_fusion.3), channel_id=1, source_target_pairs={{0,1},{1,2},{2,3},{3,4},{4,5},{5,6},{6,7},{7,8},{8,9},{9,10},{10,1... | collective-permute-start | bytes 786440 | tf_op jit(solution)/shard_map/while/body/eval_jaxpr/ppermute | solution.py:20
  226.5 20.7 %collective-permute-start = (bf16[2,256,128]{2,1,0:T(8,128)(2,1)S(1)}, bf16[2,256,128]{2,1,0:T(8,128)(2,1)S(1)}, u32[]{:S(2)}, u32[]{:S(2)}) collective-permute-start(bf16[2,256,128]{2,1,0:T(8,128)(2,1)S(1)} %copy.134), channel_id=1, source_target_pairs={{0,1},{1,2},{2,3},{3,4},{4,5},{5,6},{6,7},{7,8},{8,9},{9,10},{10,1... | collective-permute-start | bytes 393224 | tf_op jit(solution)/shard_map/while/body/eval_jaxpr/ppermute | solution.py:15
  230.5 20.8 %collective-permute-start.1 = (f32[2,256,128]{2,1,0:T(8,128)S(1)}, f32[2,256,128]{2,1,0:T(8,128)S(1)}, u32[]{:S(2)}, u32[]{:S(2)}) collective-permute-start(f32[2,256,128]{2,1,0:T(8,128)S(1)} %maximum_add_fusion.3), channel_id=1, source_target_pairs={{0,1},{1,2},{2,3},{3,4},{4,5},{5,6},{6,7},{7,8},{8,9},{9,10},{10,1... | collective-permute-start | bytes 786440 | tf_op jit(solution)/shard_map/while/body/eval_jaxpr/ppermute | solution.py:20
  251.4 19.0 %collective-permute-start = (bf16[2,256,128]{2,1,0:T(8,128)(2,1)S(1)}, bf16[2,256,128]{2,1,0:T(8,128)(2,1)S(1)}, u32[]{:S(2)}, u32[]{:S(2)}) collective-permute-start(bf16[2,256,128]{2,1,0:T(8,128)(2,1)S(1)} %copy.134), channel_id=1, source_target_pairs={{0,1},{1,2},{2,3},{3,4},{4,5},{5,6},{6,7},{7,8},{8,9},{9,10},{10,1... | collective-permute-start | bytes 393224 | tf_op jit(solution)/shard_map/while/body/eval_jaxpr/ppermute | solution.py:15
  255.3 20.5 %collective-permute-start.1 = (f32[2,256,128]{2,1,0:T(8,128)S(1)}, f32[2,256,128]{2,1,0:T(8,128)S(1)}, u32[]{:S(2)}, u32[]{:S(2)}) collective-permute-start(f32[2,256,128]{2,1,0:T(8,128)S(1)} %maximum_add_fusion.3), channel_id=1, source_target_pairs={{0,1},{1,2},{2,3},{3,4},{4,5},{5,6},{6,7},{7,8},{8,9},{9,10},{10,1... | collective-permute-start | bytes 786440 | tf_op jit(solution)/shard_map/while/body/eval_jaxpr/ppermute | solution.py:20
  275.8 18.6 %collective-permute-start = (bf16[2,256,128]{2,1,0:T(8,128)(2,1)S(1)}, bf16[2,256,128]{2,1,0:T(8,128)(2,1)S(1)}, u32[]{:S(2)}, u32[]{:S(2)}) collective-permute-start(bf16[2,256,128]{2,1,0:T(8,128)(2,1)S(1)} %copy.134), channel_id=1, source_target_pairs={{0,1},{1,2},{2,3},{3,4},{4,5},{5,6},{6,7},{7,8},{8,9},{9,10},{10,1... | collective-permute-start | bytes 393224 | tf_op jit(solution)/shard_map/while/body/eval_jaxpr/ppermute | solution.py:15
  280.2 20.6 %collective-permute-start.1 = (f32[2,256,128]{2,1,0:T(8,128)S(1)}, f32[2,256,128]{2,1,0:T(8,128)S(1)}, u32[]{:S(2)}, u32[]{:S(2)}) collective-permute-start(f32[2,256,128]{2,1,0:T(8,128)S(1)} %maximum_add_fusion.3), channel_id=1, source_target_pairs={{0,1},{1,2},{2,3},{3,4},{4,5},{5,6},{6,7},{7,8},{8,9},{9,10},{10,1... | collective-permute-start | bytes 786440 | tf_op jit(solution)/shard_map/while/body/eval_jaxpr/ppermute | solution.py:20
  304.8 19.5 %collective-permute-start.1 = (f32[2,256,128]{2,1,0:T(8,128)S(1)}, f32[2,256,128]{2,1,0:T(8,128)S(1)}, u32[]{:S(2)}, u32[]{:S(2)}) collective-permute-start(f32[2,256,128]{2,1,0:T(8,128)S(1)} %maximum_add_fusion.3), channel_id=1, source_target_pairs={{0,1},{1,2},{2,3},{3,4},{4,5},{5,6},{6,7},{7,8},{8,9},{9,10},{10,1... | collective-permute-start | bytes 786440 | tf_op jit(solution)/shard_map/while/body/eval_jaxpr/ppermute | solution.py:20
  324.2 17.7 %collective-permute-start = (bf16[2,256,128]{2,1,0:T(8,128)(2,1)S(1)}, bf16[2,256,128]{2,1,0:T(8,128)(2,1)S(1)}, u32[]{:S(2)}, u32[]{:S(2)}) collective-permute-start(bf16[2,256,128]{2,1,0:T(8,128)(2,1)S(1)} %copy.134), channel_id=1, source_target_pairs={{0,1},{1,2},{2,3},{3,4},{4,5},{5,6},{6,7},{7,8},{8,9},{9,10},{10,1... | collective-permute-start | bytes 393224 | tf_op jit(solution)/shard_map/while/body/eval_jaxpr/ppermute | solution.py:15
  328.3 21.2 %collective-permute-start.1 = (f32[2,256,128]{2,1,0:T(8,128)S(1)}, f32[2,256,128]{2,1,0:T(8,128)S(1)}, u32[]{:S(2)}, u32[]{:S(2)}) collective-permute-start(f32[2,256,128]{2,1,0:T(8,128)S(1)} %maximum_add_fusion.3), channel_id=1, source_target_pairs={{0,1},{1,2},{2,3},{3,4},{4,5},{5,6},{6,7},{7,8},{8,9},{9,10},{10,1... | collective-permute-start | bytes 786440 | tf_op jit(solution)/shard_map/while/body/eval_jaxpr/ppermute | solution.py:20
  349.5 18.5 %collective-permute-start = (bf16[2,256,128]{2,1,0:T(8,128)(2,1)S(1)}, bf16[2,256,128]{2,1,0:T(8,128)(2,1)S(1)}, u32[]{:S(2)}, u32[]{:S(2)}) collective-permute-start(bf16[2,256,128]{2,1,0:T(8,128)(2,1)S(1)} %copy.134), channel_id=1, source_target_pairs={{0,1},{1,2},{2,3},{3,4},{4,5},{5,6},{6,7},{7,8},{8,9},{9,10},{10,1... | collective-permute-start | bytes 393224 | tf_op jit(solution)/shard_map/while/body/eval_jaxpr/ppermute | solution.py:15
  389.1 18.0 %collective-permute-start = (bf16[2,256,128]{2,1,0:T(8,128)(2,1)S(1)}, bf16[2,256,128]{2,1,0:T(8,128)(2,1)S(1)}, u32[]{:S(2)}, u32[]{:S(2)}) collective-permute-start(bf16[2,256,128]{2,1,0:T(8,128)(2,1)S(1)} %copy.134), channel_id=1, source_target_pairs={{0,1},{1,2},{2,3},{3,4},{4,5},{5,6},{6,7},{7,8},{8,9},{9,10},{10,1... | collective-permute-start | bytes 393224 | tf_op jit(solution)/shard_map/while/body/eval_jaxpr/ppermute | solution.py:15
  411.3 18.5 %collective-permute-start = (bf16[2,256,128]{2,1,0:T(8,128)(2,1)S(1)}, bf16[2,256,128]{2,1,0:T(8,128)(2,1)S(1)}, u32[]{:S(2)}, u32[]{:S(2)}) collective-permute-start(bf16[2,256,128]{2,1,0:T(8,128)(2,1)S(1)} %copy.134), channel_id=1, source_target_pairs={{0,1},{1,2},{2,3},{3,4},{4,5},{5,6},{6,7},{7,8},{8,9},{9,10},{10,1... | collective-permute-start | bytes 393224 | tf_op jit(solution)/shard_map/while/body/eval_jaxpr/ppermute | solution.py:15
  421.1 17.7 %collective-permute-start.1 = (f32[2,256,128]{2,1,0:T(8,128)S(1)}, f32[2,256,128]{2,1,0:T(8,128)S(1)}, u32[]{:S(2)}, u32[]{:S(2)}) collective-permute-start(f32[2,256,128]{2,1,0:T(8,128)S(1)} %maximum_add_fusion.3), channel_id=1, source_target_pairs={{0,1},{1,2},{2,3},{3,4},{4,5},{5,6},{6,7},{7,8},{8,9},{9,10},{10,1... | collective-permute-start | bytes 786440 | tf_op jit(solution)/shard_map/while/body/eval_jaxpr/ppermute | solution.py:20
  532.8 22.3 %collective-permute-start = (bf16[2,256,128]{2,1,0:T(8,128)(2,1)S(1)}, bf16[2,256,128]{2,1,0:T(8,128)(2,1)S(1)}, u32[]{:S(2)}, u32[]{:S(2)}) collective-permute-start(bf16[2,256,128]{2,1,0:T(8,128)(2,1)S(1)} %copy.134), channel_id=1, source_target_pairs={{0,1},{1,2},{2,3},{3,4},{4,5},{5,6},{6,7},{7,8},{8,9},{9,10},{10,1... | collective-permute-start | bytes 393224 | tf_op jit(solution)/shard_map/while/body/eval_jaxpr/ppermute | solution.py:15
  543.2 21.6 %collective-permute-start.1 = (f32[2,256,128]{2,1,0:T(8,128)S(1)}, f32[2,256,128]{2,1,0:T(8,128)S(1)}, u32[]{:S(2)}, u32[]{:S(2)}) collective-permute-start(f32[2,256,128]{2,1,0:T(8,128)S(1)} %maximum_add_fusion.3), channel_id=1, source_target_pairs={{0,1},{1,2},{2,3},{3,4},{4,5},{5,6},{6,7},{7,8},{8,9},{9,10},{10,1... | collective-permute-start | bytes 786440 | tf_op jit(solution)/shard_map/while/body/eval_jaxpr/ppermute | solution.py:20
  595.8 20.4 %collective-permute-start.1 = (f32[2,256,128]{2,1,0:T(8,128)S(1)}, f32[2,256,128]{2,1,0:T(8,128)S(1)}, u32[]{:S(2)}, u32[]{:S(2)}) collective-permute-start(f32[2,256,128]{2,1,0:T(8,128)S(1)} %maximum_add_fusion.3), channel_id=1, source_target_pairs={{0,1},{1,2},{2,3},{3,4},{4,5},{5,6},{6,7},{7,8},{8,9},{9,10},{10,1... | collective-permute-start | bytes 786440 | tf_op jit(solution)/shard_map/while/body/eval_jaxpr/ppermute | solution.py:20
  699.1 22.1 %collective-permute-start.1 = (f32[2,256,128]{2,1,0:T(8,128)S(1)}, f32[2,256,128]{2,1,0:T(8,128)S(1)}, u32[]{:S(2)}, u32[]{:S(2)}) collective-permute-start(f32[2,256,128]{2,1,0:T(8,128)S(1)} %maximum_add_fusion.3), channel_id=1, source_target_pairs={{0,1},{1,2},{2,3},{3,4},{4,5},{5,6},{6,7},{7,8},{8,9},{9,10},{10,1... | collective-permute-start | bytes 786440 | tf_op jit(solution)/shard_map/while/body/eval_jaxpr/ppermute | solution.py:20
  760.9 18.6 %collective-permute-start = (bf16[2,256,128]{2,1,0:T(8,128)(2,1)S(1)}, bf16[2,256,128]{2,1,0:T(8,128)(2,1)S(1)}, u32[]{:S(2)}, u32[]{:S(2)}) collective-permute-start(bf16[2,256,128]{2,1,0:T(8,128)(2,1)S(1)} %copy.134), channel_id=1, source_target_pairs={{0,1},{1,2},{2,3},{3,4},{4,5},{5,6},{6,7},{7,8},{8,9},{9,10},{10,1... | collective-permute-start | bytes 393224 | tf_op jit(solution)/shard_map/while/body/eval_jaxpr/ppermute | solution.py:15
  764.9 23.4 %collective-permute-start.1 = (f32[2,256,128]{2,1,0:T(8,128)S(1)}, f32[2,256,128]{2,1,0:T(8,128)S(1)}, u32[]{:S(2)}, u32[]{:S(2)}) collective-permute-start(f32[2,256,128]{2,1,0:T(8,128)S(1)} %maximum_add_fusion.3), channel_id=1, source_target_pairs={{0,1},{1,2},{2,3},{3,4},{4,5},{5,6},{6,7},{7,8},{8,9},{9,10},{10,1... | collective-permute-start | bytes 786440 | tf_op jit(solution)/shard_map/while/body/eval_jaxpr/ppermute | solution.py:20
  792.2 18.0 %collective-permute-start.1 = (f32[2,256,128]{2,1,0:T(8,128)S(1)}, f32[2,256,128]{2,1,0:T(8,128)S(1)}, u32[]{:S(2)}, u32[]{:S(2)}) collective-permute-start(f32[2,256,128]{2,1,0:T(8,128)S(1)} %maximum_add_fusion.3), channel_id=1, source_target_pairs={{0,1},{1,2},{2,3},{3,4},{4,5},{5,6},{6,7},{7,8},{8,9},{9,10},{10,1... | collective-permute-start | bytes 786440 | tf_op jit(solution)/shard_map/while/body/eval_jaxpr/ppermute | solution.py:20
  814.1 19.4 %collective-permute-start.1 = (f32[2,256,128]{2,1,0:T(8,128)S(1)}, f32[2,256,128]{2,1,0:T(8,128)S(1)}, u32[]{:S(2)}, u32[]{:S(2)}) collective-permute-start(f32[2,256,128]{2,1,0:T(8,128)S(1)} %maximum_add_fusion.3), channel_id=1, source_target_pairs={{0,1},{1,2},{2,3},{3,4},{4,5},{5,6},{6,7},{7,8},{8,9},{9,10},{10,1... | collective-permute-start | bytes 786440 | tf_op jit(solution)/shard_map/while/body/eval_jaxpr/ppermute | solution.py:20
  (53 other events, 813.9 us)
